TPU v7x, 32 devices: a whole 2x2x4 slice. The times are simulated.
32 devices in a mesh: rows: 2 (over x), cent: 16 (over z, y, core).
Axes of the slice: x: 2, y: 2, z: 4, core: 2. Of those that a mesh axis runs over, the one named last changes fastest.
Arguments:
- embeddings: bfloat16 [2048, 768], P(('rows', 'cent')), may hold values from -33 to 33
- centroids: bfloat16 [2048, 768], P('cent'), may hold values from -4 to 4
- group_length: int32 [2], P('rows'), may hold values from 256 to 1024, as said below
Outputs:
- new_centroids: bfloat16 [2048, 768], P('cent')
- new_moments: bfloat16 [2048, 768], P('cent')
- loglik: float32 [2048], P(('rows', 'cent'))
Inputs may be any that keep to these rules, and one draw needn't show every extreme that they name: Row group g uses its first group_length[g] of its 1024 row slots; at least one group uses all of them.
All inputs are finite; a program needn't handle non-finite values.
Results may differ from a plain program's by a relative error of at most 0.0047.
Values may be sent and summed in bfloat16 or wider, within the bound.
A program may use at most 64 MiB of HBM per device.

v0:
```python
import math
import jax
import jax.numpy as jnp
from jax import lax
from jax.sharding import PartitionSpec as P

score_factor = 3.0
prior_weight = 1.0
contract_rows = (((0,), (0,)), ((), ()))
contract_width = (((1,), (1,)), ((), ()))


def combined_all(part, axis, combine):
    gathered = jax.tree.map(lambda a: lax.all_gather(a, axis), part)

    def take(source):
        return jax.tree.map(lambda a: lax.dynamic_index_in_dim(a, source, 0, False), gathered)

    return lax.fori_loop(
        1, lax.axis_size(axis), lambda source, state: combine(state, take(source)), take(0)
    )


def scores(row_block, centroid_rows, squared_norm, factor):
    inner = lax.dot_general(
        row_block, centroid_rows, contract_width, preferred_element_type=jnp.float32
    )
    return factor * (inner - 0.5 * squared_norm[None, :])


def finish_totals(peaks, exp_sums):

    def combine(left_part, right_part):
        highest = jnp.maximum(left_part[0], right_part[0])
        joined = left_part[1] * jnp.exp(left_part[0] - highest) + right_part[1] * jnp.exp(
            right_part[0] - highest
        )
        return (highest, joined)

    peak_all, total_all = combined_all((peaks, exp_sums), "cent", combine)
    return peak_all + jnp.log(total_all)


def add_stats(row_piece, logits, piece_lse, valid_rows):
    responsibility = jnp.where(
        valid_rows[:, None], jnp.exp(logits - piece_lse[:, None]), 0.0
    ).astype(jnp.bfloat16)
    rows_wide = row_piece.astype(jnp.float32)
    squares = (rows_wide * rows_wide).astype(jnp.bfloat16)
    weighted = lax.dot_general(
        responsibility, row_piece, contract_rows, preferred_element_type=jnp.float32
    )
    moments = lax.dot_general(
        responsibility, squares, contract_rows, preferred_element_type=jnp.float32
    )
    weight_mass = jnp.sum(responsibility.astype(jnp.float32), axis=0)
    return (weighted, moments, weight_mass)


def shards(embeddings, centroids, group_length):
    row_count = embeddings.shape[0]
    width = embeddings.shape[1]
    factor = score_factor / math.sqrt(width)
    cent_wide = centroids.astype(jnp.float32)
    squared_norm = jnp.sum(cent_wide * cent_wide, axis=1)
    used_rows = group_length[0]
    offset = lax.axis_index("cent") * row_count
    own_positions = offset + jnp.arange(row_count, dtype=jnp.int32)
    own_valid = own_positions < used_rows
    logits = scores(
        lax.all_gather(embeddings, "cent", axis=0, tiled=True), centroids, squared_norm, factor
    )
    piece_peak = jnp.max(logits, axis=1)
    piece_total = jnp.sum(jnp.exp(logits - piece_peak[:, None]), axis=1)
    peaks = piece_peak
    exp_sums = piece_total
    peaks, exp_sums = (peaks, exp_sums)
    group_lse = finish_totals(peaks, exp_sums)
    row_piece = lax.all_gather(embeddings, "cent", axis=0, tiled=True)
    piece_count = row_piece.shape[0]
    logits = scores(row_piece, centroids, squared_norm, factor)
    positions = jnp.arange(piece_count, dtype=jnp.int32)
    weighted, moments, weight_mass = add_stats(row_piece, logits, group_lse, positions < used_rows)
    own_lse = lax.dynamic_slice_in_dim(group_lse, offset, row_count, 0)
    weighted, moments, weight_mass = lax.psum((weighted, moments, weight_mass), "rows")
    denominator = weight_mass[:, None] + prior_weight
    new_centroids = ((weighted + prior_weight * cent_wide) / denominator).astype(jnp.bfloat16)
    new_moments = ((moments + prior_weight) / denominator).astype(jnp.bfloat16)
    loglik = jnp.where(own_valid, own_lse, jnp.zeros_like(own_lse))
    return (new_centroids, new_moments, loglik)


def solution(mesh):
    return jax.shard_map(
        shards,
        mesh=mesh,
        in_specs=(P(("rows", "cent"), None), P("cent", None), P("rows")),
        out_specs=(P("cent", None), P("cent", None), P(("rows", "cent"))),
        check_vma=False,
    )
```

profile of v0, /device:TPU:0, one launch (start us, length us, event | category | flops | bytes accessed | tf_op | source)
XLA Modules:
  0.0 137.1 jit_solution(16626521679384497014)
XLA Ops:
  7.2 0.0 all-gather.4.cloned.1.call-start
  7.2 0.7 all-gather.4.cloned.1.call-update
  7.9 0.0 all-reduce.3.cloned.1.call-start
  8.6 1.0 fusion.2
  9.7 43.0 %all-gather.4.cloned.1.call-done = bf16[1024,768]{1,0:T(8,128)(2,1)} async-done(((bf16[64,768]{1,0:T(8,128)(2,1)}), bf16[1024,768]{1,0:T(8,128)(2,1)}) %all-gather.4.cloned.1.call-update) | async-done | bytes 1572880 | tf_op jit(solution)/shard_map/all_gather | solution.py:79
  52.6 2.1 %fusion.5 = (f32[1024]{0:T(1024)S(1)}, f32[1024,128]{0,1:T(8,128)S(1)}) fusion(f32[128]{0:T(128)S(1)} %broadcast_multiply_fusion, bf16[1024,768]{1,0:T(8,128)(2,1)} %all-gather.4.cloned.1.call-done, bf16[128,768]{1,0:T(8,128)(2,1)} %param.6), kind=kOutput, calls=%fused_computation.21 | convolution fusion | flops 201718784 | bytes 2298368 | tf_op jit(solution)/shard_map/dot_general | solution.py:25
  54.7 0.0 copy-start
  54.7 19.4 %all-gather = f32[16384]{0:T(1024)S(1)} all-gather(f32[1024]{0:T(1024)S(1)} %get-tuple-element.158), channel_id=2, replica_groups=mesh['rows'=2,'cent'=16] {'cent'}, dimensions={0}, use_global_device_ids=true | all-gather | bytes 69632 | tf_op jit(solution)/shard_map/all_gather | solution.py:14
  74.1 0.1 exponential_reduce_fusion
  74.2 17.6 %all-gather.1 = f32[16384]{0:T(1024)S(1)} all-gather(f32[1024]{0:T(1024)S(1)} %exponential_reduce_fusion), channel_id=3, replica_groups=mesh['rows'=2,'cent'=16] {'cent'}, dimensions={0}, use_global_device_ids=true | all-gather | bytes 69632 | tf_op jit(solution)/shard_map/all_gather | solution.py:14
  91.9 0.9 while.17
  92.8 0.2 convert_reduce_fusion
  93.0 0.0 copy-done
  93.0 1.2 fusion
  94.2 0.0 copy-start.1
  94.2 1.1 fusion.6
  95.3 0.0 all-reduce.3.cloned.1.call-update
  95.4 4.9 %psum.22 = f32[128]{0:T(128)S(1)} all-reduce(f32[128]{0:T(128)S(1)} %get-tuple-element.152), channel_id=1, replica_groups=mesh['rows'=2,'cent'=16] {'rows'}, use_global_device_ids=true, to_apply=%region_7.8 | all-reduce | flops 128 | bytes 1024 | tf_op jit(solution)/shard_map/psum | solution.py:85
  100.3 0.6 compare_select_fusion
  100.9 27.3 %all-reduce.3.cloned.1.call-done = (f32[128,768]{1,0:T(8,128)}, f32[128,768]{1,0:T(8,128)}) async-done(((f32[128,768]{1,0:T(8,128)}, f32[128,768]{1,0:T(8,128)}), (f32[128,768]{1,0:T(8,128)}, f32[128,768]{1,0:T(8,128)})) %all-reduce.3.cloned.1.call-update) | async-done | bytes 786448 | tf_op jit(solution)/shard_map/psum | solution.py:85
  128.2 0.0 copy-done.1
  128.2 2.0 %divide_convert_fusion = (bf16[128,768]{1,0:T(8,128)(2,1)}, bf16[128,768]{1,0:T(8,128)(2,1)}) fusion(f32[128,768]{1,0:T(8,128)} %get-tuple-element.149, f32[128]{0:T(128)S(1)} %broadcast_add_fusion, f32[128,768]{1,0:T(8,128)} %get-tuple-element.148, bf16[128,768]{1,0:T(8,128)(2,1)S(1)} %copy-done.1), kind=kLoop, calls=%fused_computation.15 | loop fusion | flops 688128 | bytes 1376768 | tf_op jit(solution)/shard_map/convert_element_type | solution.py:88
  (38 shorter events, 0.5 us)
Async XLA Ops:
  7.2 45.4 %all-gather.4.cloned.1.call-start = ((), (), s32[]{:S(2)}) async-start(), calls=%async_computation | async-start | bytes 1671168 | tf_op jit(solution)/shard_map/all_gather | solution.py:79
  7.9 120.3 %all-reduce.3.cloned.1.call-start = ((), (), s32[]{:S(2)}) async-start(), calls=%async_computation.1 | async-start | bytes 1572864 | tf_op jit(solution)/shard_map/psum | solution.py:85
  54.7 38.3 %copy-start = (bf16[1024,768]{1,0:T(8,128)(2,1)S(1)}, bf16[1024,768]{1,0:T(8,128)(2,1)}, u32[]{:S(2)}) copy-start(bf16[1024,768]{1,0:T(8,128)(2,1)} %all-gather.4.cloned.1.call-done) | copy-start | bytes 4718596
  94.2 34.0 %copy-start.1 = (bf16[128,768]{1,0:T(8,128)(2,1)S(1)}, bf16[128,768]{1,0:T(8,128)(2,1)}, u32[]{:S(2)}) copy-start(bf16[128,768]{1,0:T(8,128)(2,1)} %param.6) | copy-start | bytes 589828
Sparse Core Ops, SparseCore 0:
  10.3 42.3 all-gather.3
  95.5 32.7 all-reduce.2
where the time goes:
time: 137 us
  waiting for transfers between devices  71 us (52%)
  blocking collectives  42 us (31%)
  between operations  14.7 us (11%)
  matrix products  4.43 us (3%)
  other arithmetic  4.09 us (3%)
    all_gather x1, waiting for transfers between devices, shards(): row_piece = lax.all_gather(embeddings, 'cent', axis=0, tiled=True)  43 us
    all_gather x2, blocking collectives, combined_all(): gathered = jax.tree.map(lambda a: lax.all_gather(a, axis), part)  37 us
    psum x1, waiting for transfers between devices, shards(): lax.psum((weighted, moments, weight_mass), 'rows')  27.3 us
    psum x1, blocking collectives, shards(): lax.psum((weighted, moments, weight_mass), 'rows')  4.93 us
  transfers between devices with their start and end apart: 2, of which 2 were waited for; matrix products, arithmetic and copies ran while one was open for 1% of the time, Pallas kernels for 0%

commit v1 on v0

--- a/solution.py
+++ b/solution.py
@@ -76,7 +76,8 @@
     exp_sums = piece_total
     peaks, exp_sums = (peaks, exp_sums)
     group_lse = finish_totals(peaks, exp_sums)
-    row_piece = lax.all_gather(embeddings, "cent", axis=0, tiled=True)
+    repeated = jnp.stack([embeddings] * lax.axis_size("cent"))
+    row_piece = jnp.concatenate(lax.all_to_all(repeated, "cent", 0, 0), axis=0)
     piece_count = row_piece.shape[0]
     logits = scores(row_piece, centroids, squared_norm, factor)
     positions = jnp.arange(piece_count, dtype=jnp.int32)

time: 137 us -> 155 us (1.13)
  starting transfers between devices: 0.08 us -> 7.62 us
  waiting for transfers between devices: 71 us -> 77.6 us
  local copies, waits for them, and re-layouts: 0.27 us -> 2.46 us
    all_to_all x0 -> x1, starting transfers between devices: none -> 7.55 us  [shards(): row_piece = jnp.concatenate(lax.all_to_all(repeated, 'cent', 0, 0), axis=0)]
    all_gather x1, waiting for transfers between devices: 43 us -> 49.5 us  [shards(): lax.all_gather(embeddings, 'cent', axis=0, tiled=True)]
    another operation x0 -> x1, local copies, waits for them, and re-layouts: none -> 2.2 us  [shards(): repeated = jnp.stack([embeddings] * lax.axis_size('cent'))]
  transfers between devices with their start and end apart: 2 -> 3, of which waited for: 2 -> 2; matrix products, arithmetic and copies ran while one was open for 1% -> 4% of each run, Pallas kernels for 0% -> 0%
where the time goes in v1:
time: 155 us
  waiting for transfers between devices  77.6 us (50%)
  blocking collectives  43.4 us (28%)
  between operations  14.8 us (10%)
  starting transfers between devices  7.62 us (5%)
  matrix products  5.02 us (3%)
  other arithmetic  3.27 us (2%)
  local copies, waits for them, and re-layouts  2.46 us (2%)
    all_gather x1, waiting for transfers between devices, shards(): lax.all_gather(embeddings, 'cent', axis=0, tiled=True)  49.5 us
    all_gather x2, blocking collectives, combined_all(): gathered = jax.tree.map(lambda a: lax.all_gather(a, axis), part)  38.5 us
    psum x1, waiting for transfers between devices, shards(): lax.psum((weighted, moments, weight_mass), 'rows')  27.4 us
    all_to_all x1, starting transfers between devices, shards(): row_piece = jnp.concatenate(lax.all_to_all(repeated, 'cent', 0, 0), axis=0)  7.55 us
    psum x1, blocking collectives, shards(): lax.psum((weighted, moments, weight_mass), 'rows')  4.93 us
  transfers between devices with their start and end apart: 3, of which 2 were waited for; matrix products, arithmetic and copies ran while one was open for 4% of the time, Pallas kernels for 0%

profile of v1, /device:TPU:0, one launch (start us, length us, event | category | flops | bytes accessed | tf_op | source)
XLA Modules:
  0.0 154.6 jit_solution(13595821174738202462)
XLA Ops:
  7.2 0.0 all-gather.4.cloned.1.call-start
  7.2 0.7 all-gather.4.cloned.1.call-update
  7.9 2.2 %stack.2 = bf16[16,64,768]{2,1,0:T(8,128)(2,1)} broadcast(bf16[64,768]{1,0:T(8,128)(2,1)} %param.5), dimensions={1,2} | broadcast | bytes 1671168 | tf_op jit(solution)/shard_map/stack | solution.py:79
  10.1 0.0 copy-start
  10.1 7.5 %all-to-all-start = ((bf16[16,64,768]{2,1,0:T(8,128)(2,1)}), bf16[16,64,768]{2,1,0:T(8,128)(2,1)S(1)}, u32[]{:S(2)}, u32[]{:S(2)}) async-start(bf16[16,64,768]{2,1,0:T(8,128)(2,1)} %stack.2), calls=%async_computation | async-start | bytes 3145728 | tf_op jit(solution)/shard_map/all_to_all | solution.py:80
  17.6 0.0 all-reduce.3.cloned.1.call-start
  18.4 0.0 copy-done
  18.4 0.1 fusion.7
  18.5 49.5 %all-gather.4.cloned.1.call-done = bf16[1024,768]{1,0:T(8,128)(2,1)} async-done(((bf16[64,768]{1,0:T(8,128)(2,1)}), bf16[1024,768]{1,0:T(8,128)(2,1)}) %all-gather.4.cloned.1.call-update) | async-done | bytes 1572880 | tf_op jit(solution)/shard_map/all_gather | solution.py:71
  68.0 2.1 %fusion.10 = (f32[1024]{0:T(1024)S(1)}, f32[1024,128]{1,0:T(8,128)S(1)}) fusion(f32[128]{0:T(128)S(1)} %broadcast_multiply_fusion, bf16[1024,768]{1,0:T(8,128)(2,1)} %all-gather.4.cloned.1.call-done, bf16[128,768]{1,0:T(8,128)(2,1)S(1)} %copy-done), kind=kOutput, calls=%fused_computation.26 | convolution fusion | flops 201718784 | bytes 2298368 | tf_op jit(solution)/shard_map/dot_general | solution.py:25
  70.0 0.4 exponential_reduce_fusion
  70.4 20.9 %all-gather.1 = f32[16384]{0:T(1024)S(1)} all-gather(f32[1024]{0:T(1024)S(1)} %exponential_reduce_fusion), channel_id=3, replica_groups=mesh['rows'=2,'cent'=16] {'cent'}, dimensions={0}, use_global_device_ids=true | all-gather | bytes 69632 | tf_op jit(solution)/shard_map/all_gather | solution.py:14
  91.3 17.6 %all-gather = f32[16384]{0:T(1024)S(1)} all-gather(f32[1024]{0:T(1024)S(1)} %get-tuple-element.156), channel_id=2, replica_groups=mesh['rows'=2,'cent'=16] {'cent'}, dimensions={0}, use_global_device_ids=true | all-gather | bytes 69632 | tf_op jit(solution)/shard_map/all_gather | solution.py:14
  108.9 0.9 while.17
  109.9 0.0 all-to-all-done
  109.9 0.6 convert_reduce_fusion
  110.5 1.2 fusion
  111.7 1.2 fusion.11
  112.8 0.0 all-reduce.3.cloned.1.call-update
  112.9 4.9 %psum.22 = f32[128]{0:T(128)S(1)} all-reduce(f32[128]{0:T(128)S(1)} %get-tuple-element.158), channel_id=1, replica_groups=mesh['rows'=2,'cent'=16] {'rows'}, use_global_device_ids=true, to_apply=%region_7.8 | all-reduce | flops 128 | bytes 1024 | tf_op jit(solution)/shard_map/psum | solution.py:86
  117.8 0.6 compare_select_fusion
  118.4 27.4 %all-reduce.3.cloned.1.call-done = (f32[128,768]{1,0:T(8,128)}, f32[128,768]{1,0:T(8,128)}) async-done(((f32[128,768]{1,0:T(8,128)}, f32[128,768]{1,0:T(8,128)}), (f32[128,768]{1,0:T(8,128)}, f32[128,768]{1,0:T(8,128)})) %all-reduce.3.cloned.1.call-update) | async-done | bytes 786448 | tf_op jit(solution)/shard_map/psum | solution.py:86
  145.8 2.0 %divide_convert_fusion = (bf16[128,768]{1,0:T(8,128)(2,1)}, bf16[128,768]{1,0:T(8,128)(2,1)}) fusion(f32[128,768]{1,0:T(8,128)} %get-tuple-element.149, f32[128]{0:T(128)S(1)} %broadcast_add_fusion, f32[128,768]{1,0:T(8,128)} %get-tuple-element.148, bf16[128,768]{1,0:T(8,128)(2,1)S(1)} %copy-done), kind=kLoop, calls=%fused_computation.20 | loop fusion | flops 688128 | bytes 1376768 | tf_op jit(solution)/shard_map/convert_element_type | solution.py:89
  (38 shorter events, 0.5 us)
Async XLA Ops:
  7.2 60.8 %all-gather.4.cloned.1.call-start = ((), (), s32[]{:S(2)}) async-start(), calls=%async_computation.1 | async-start | bytes 1671168 | tf_op jit(solution)/shard_map/all_gather | solution.py:71
  10.1 8.3 %copy-start = (bf16[128,768]{1,0:T(8,128)(2,1)S(1)}, bf16[128,768]{1,0:T(8,128)(2,1)}, u32[]{:S(2)}) copy-start(bf16[128,768]{1,0:T(8,128)(2,1)} %param.6) | copy-start | bytes 589828
  10.1 99.8 %all-to-all-start = ((bf16[16,64,768]{2,1,0:T(8,128)(2,1)}), bf16[16,64,768]{2,1,0:T(8,128)(2,1)S(1)}, u32[]{:S(2)}, u32[]{:S(2)}) async-start(bf16[16,64,768]{2,1,0:T(8,128)(2,1)} %stack.2), calls=%async_computation | async-start | bytes 3145728 | tf_op jit(solution)/shard_map/all_to_all | solution.py:80
  17.6 128.1 %all-reduce.3.cloned.1.call-start = ((), (), s32[]{:S(2)}) async-start(), calls=%async_computation.2 | async-start | bytes 1572864 | tf_op jit(solution)/shard_map/psum | solution.py:86
Sparse Core Ops, SparseCore 0:
  10.3 57.6 all-gather.3
  113.0 32.7 all-reduce.2
